TPU v7x, 256 devices: a whole 4x4x8 slice. The times are simulated.
256 devices in a mesh: blk: 16 (over y, x_lo, core), head: 16 (over z, x_hi).
Axes of the slice: x: 4 (x_hi: 2, x_lo: 2; x = x_hi * 2 + x_lo), y: 4, z: 8, core: 2. Of those that a mesh axis runs over, the one named last changes fastest.
Arguments:
- queries: bfloat16 [32768, 2048], P(('blk', 'head')), may hold values from -6 to 6
- keys: bfloat16 [32768, 2048], P(('blk', 'head')), may hold values from -6 to 6
- values: bfloat16 [32768, 2048], P(('blk', 'head')), may hold values from -6 to 6
- slopes: float32 [16], replicated, may hold values from 0.02 to 0.4
- frames: int32 [32768], replicated, may hold values from 0 to 127, never falling along the last dimension, each value on 1 to 512 neighbouring positions
- block_list: int32 [16, 256, 32], replicated, may hold values from 0 to 255, as said below
Outputs:
- attended: bfloat16 [32768, 2048], P(('blk', 'head'))
Inputs may be any that keep to these rules, and one draw needn't show every extreme that they name: `block_list`: each row lists 32 distinct block columns, among them the row's own block and the block 128 away, counted round.
All inputs are finite; a program needn't handle non-finite values.
Results may differ from a plain program's by a relative error of at most 0.0065.
Values may be sent and summed in bfloat16 or wider, within the bound.
A program may use at most 128 MiB of HBM per device.

v0:
```python
import jax
import jax.numpy as jnp
from jax import lax
from jax.sharding import PartitionSpec as P

HD = 128
HEADS = 16
BLOCK = 128


def pick_tile(tiles, column):
    return tiles[column]


def per_device(queries, keys, values, slopes, frames, block_list):
    heads_dev = HEADS // lax.axis_size("head")
    query_group, key_group, value_group = (
        lax.all_to_all(queries, "head", split_axis=1, concat_axis=0, tiled=True),
        lax.all_to_all(keys, "head", split_axis=1, concat_axis=0, tiled=True),
        lax.all_to_all(values, "head", split_axis=1, concat_axis=0, tiled=True),
    )
    group_rows = query_group.shape[0]
    group_blocks = group_rows // BLOCK
    list_width = block_list.shape[2]
    group_start = lax.axis_index("blk") * group_rows
    head_start = lax.axis_index("head") * heads_dev
    my_slopes = lax.dynamic_slice_in_dim(slopes, head_start, heads_dev)
    my_lists = lax.dynamic_slice_in_dim(block_list, head_start, heads_dev, 0)
    row_lists = lax.dynamic_slice_in_dim(my_lists, group_start // BLOCK, group_blocks, 1)
    query_heads = query_group.reshape(group_rows, heads_dev, HD)
    query_frames = lax.dynamic_slice_in_dim(frames, group_start, group_rows)
    query_blocks = query_heads.reshape(group_blocks, BLOCK, heads_dev, HD).transpose(2, 0, 1, 3)
    frame_row_index = query_frames.reshape(group_blocks, BLOCK)
    start_carry = (
        jnp.full((heads_dev, group_blocks, BLOCK), -1e30, jnp.float32),
        jnp.zeros((heads_dev, group_blocks, BLOCK), jnp.float32),
        jnp.zeros((heads_dev, group_blocks, BLOCK, HD), jnp.float32),
    )
    key_piece = lax.all_gather(key_group, "blk", axis=0, tiled=True)
    value_piece = lax.all_gather(value_group, "blk", axis=0, tiled=True)
    count = key_piece.shape[0]
    piece_blocks = count // BLOCK
    slots = min(list_width, piece_blocks)
    valid = (row_lists >= 0) & (row_lists < piece_blocks)
    position = jnp.arange(list_width, dtype=jnp.int32)
    rank = jnp.where(valid, list_width - position, 0)
    ordered, order = lax.top_k(rank, slots)
    hit_cols = jnp.clip(jnp.take_along_axis(row_lists, order, axis=2), 0, piece_blocks - 1)
    hit_ok = ordered > 0
    hits = jnp.max(jnp.sum(hit_ok.astype(jnp.int32), axis=2))
    key_block_tiles = key_piece.reshape(piece_blocks, BLOCK, heads_dev, HD).transpose(2, 0, 1, 3)
    value_tiles = value_piece.reshape(piece_blocks, BLOCK, heads_dev, HD).transpose(2, 0, 1, 3)
    key_frames = frames.reshape(piece_blocks, BLOCK)

    def one_slot(slot, state):
        run_max, run_sum, run_acc = state
        column = lax.dynamic_index_in_dim(hit_cols, slot, 2, keepdims=False)
        usable = lax.dynamic_index_in_dim(hit_ok, slot, 2, keepdims=False)
        keys_now = jax.vmap(pick_tile)(key_block_tiles, column)
        current_values = jax.vmap(pick_tile)(value_tiles, column)
        frames_now = key_frames[column]
        gap = jnp.abs(frame_row_index[None, :, :, None] - frames_now[:, :, None, :]).astype(
            jnp.float32
        )
        block_scores = jnp.einsum(
            "hgqd,hgkd->hgqk", query_blocks, keys_now, preferred_element_type=jnp.float32
        )
        block_scores = block_scores * HD ** (-0.5) - my_slopes[:, None, None, None] * gap
        flag = usable[:, :, None]
        new_max = jnp.where(flag, jnp.maximum(run_max, jnp.max(block_scores, axis=3)), run_max)
        weights = jnp.where(flag[..., None], jnp.exp(block_scores - new_max[..., None]), 0.0)
        shrink = jnp.exp(run_max - new_max)
        run_sum = run_sum * shrink + jnp.sum(weights, axis=3)
        added = jnp.einsum(
            "hgqk,hgkd->hgqd",
            weights.astype(jnp.bfloat16),
            current_values,
            preferred_element_type=jnp.float32,
        )
        run_acc = run_acc * shrink[..., None] + added
        return (new_max, run_sum, run_acc)

    run_max, run_sum, run_acc = lax.fori_loop(0, hits, one_slot, start_carry)
    normed = (run_acc / run_sum[..., None]).reshape(heads_dev, group_rows, HD)
    output = normed.astype(jnp.bfloat16).transpose(1, 0, 2).reshape(group_rows, heads_dev * HD)
    return lax.all_to_all(output, "head", split_axis=0, concat_axis=1, tiled=True)


def solution(mesh):
    placed = (
        P(("blk", "head"), None),
        P(("blk", "head"), None),
        P(("blk", "head"), None),
        P(),
        P(),
        P(),
    )
    return jax.shard_map(
        per_device, mesh=mesh, in_specs=placed, out_specs=P(("blk", "head"), None), check_vma=False
    )
```

profile of v0, /device:TPU:1, one launch (start us, length us, event | category | flops | bytes accessed | tf_op | source)
XLA Modules:
  0.0 572.4 jit_solution(10765497709024923693)
XLA Ops:
  8.2 28.7 %all_to_all.70 = bf16[128,16,128]{2,0,1:T(8,128)(2,1)} all-to-all(bf16[128,16,128]{2,0,1:T(8,128)(2,1)S(1)} %copy.29), channel_id=1, replica_groups=mesh['blk'=16,'head'=16] {'head'}, dimensions={1} | all-to-all | bytes 1048576 | tf_op jit(solution)/shard_map/all_to_all | solution.py:19
  38.6 21.8 %all_to_all.71 = bf16[128,16,128]{2,0,1:T(8,128)(2,1)} all-to-all(bf16[128,16,128]{2,0,1:T(8,128)(2,1)S(1)} %copy.32), channel_id=1, replica_groups=mesh['blk'=16,'head'=16] {'head'}, dimensions={1} | all-to-all | bytes 1048576 | tf_op jit(solution)/shard_map/all_to_all | solution.py:20
  62.5 4.8 all-to-all-start.1
  74.0 10.5 %all-to-all-done.1 = bf16[128,16,128]{0,2,1:T(8,128)(2,1)S(1)} async-done(((bf16[128,16,128]{0,2,1:T(8,128)(2,1)}), bf16[128,16,128]{0,2,1:T(8,128)(2,1)S(1)}, u32[]{:S(2)}, u32[]{:S(2)}) %all-to-all-start.1) | async-done | bytes 524320 | tf_op jit(solution)/shard_map/all_to_all | solution.py:18
  84.8 14.7 %all-gather.3.cloned.1.call-done = bf16[32768,128]{1,0:T(8,128)(2,1)} async-done(((bf16[2048,128]{1,0:T(8,128)(2,1)}), bf16[32768,128]{1,0:T(8,128)(2,1)}) %all-gather.3.cloned.1.call-update) | async-done | bytes 8388624 | tf_op jit(solution)/shard_map/all_gather | solution.py:39
  99.5 57.4 %all-gather.5.cloned.1.call-done = bf16[32768,128]{1,0:T(8,128)(2,1)} async-done(((bf16[2048,128]{1,0:T(8,128)(2,1)}), bf16[32768,128]{1,0:T(8,128)(2,1)}) %all-gather.5.cloned.1.call-update) | async-done | bytes 8388624 | tf_op jit(solution)/shard_map/all_gather | solution.py:40
  156.9 380.7 %while.14 = (s32[]{:T(128)}, f32[1,16,128]{2,1,0:T(8,128)S(1)}, f32[1,16,128]{2,1,0:T(8,128)S(1)}, f32[1,16,128,128]{3,2,1,0:T(8,128)S(1)}, s32[]{:T(128)}, /*in...) while((s32[]{:T(128)}, f32[1,16,128]{2,1,0:T(8,128)S(1)}, ...), condition=%wide.region_6.7_spmd, body=%wide.region_3.6_spmd.sunk | while | flops 138159280 | bytes 9082135 | solution.py:83
  163.7 4.0 gather_fusion.2
  175.6 4.0 gather_fusion.2
  187.4 4.0 gather_fusion.2
  199.3 4.0 gather_fusion.2
  211.2 4.0 gather_fusion.2
  223.1 4.0 gather_fusion.2
  235.0 4.0 gather_fusion.2
  246.8 4.0 gather_fusion.2
  258.7 4.0 gather_fusion.2
  270.6 4.0 gather_fusion.2
  294.4 4.0 gather_fusion.2
  306.2 4.0 gather_fusion.2
  318.1 4.0 gather_fusion.2
  330.0 4.0 gather_fusion.2
  341.9 4.0 gather_fusion.2
  353.8 4.0 gather_fusion.2
  538.0 26.7 %all_to_all.72 = bf16[16,128,128]{2,1,0:T(8,128)(2,1)S(1)} all-to-all(bf16[16,128,128]{2,1,0:T(8,128)(2,1)S(1)} %fusion.12), channel_id=1, replica_groups=mesh['blk'=16,'head'=16] {'head'}, dimensions={0} | all-to-all | bytes 1048576 | tf_op jit(solution)/shard_map/all_to_all | solution.py:86
  (498 shorter events, 307.8 us)
Async XLA Ops:
  6.5 92.9 %all-gather.3.cloned.1.call-start = ((), (), s32[]{:S(2)}) async-start(), calls=%async_computation.4 | async-start | bytes 8912896 | tf_op jit(solution)/shard_map/all_gather | solution.py:39
  8.1 64.5 %copy-start.1 = (f32[16]{0:T(128)S(1)}, f32[16]{0:T(128)}, u32[]{:S(2)}) copy-start(f32[16]{0:T(128)} %param.11) | copy-start | bytes 196
  8.2 65.8 %copy-start = (s32[32768]{0:T(1024)S(1)}, s32[32768]{0:T(1024)}, u32[]{:S(2)}) copy-start(s32[32768]{0:T(1024)} %param.12) | copy-start | bytes 393220
  36.9 119.9 %all-gather.5.cloned.1.call-start = ((), (), s32[]{:S(2)}) async-start(), calls=%async_computation.5 | async-start | bytes 8912896 | tf_op jit(solution)/shard_map/all_gather | solution.py:40
  62.5 22.0 %all-to-all-start.1 = ((bf16[128,16,128]{0,2,1:T(8,128)(2,1)}), bf16[128,16,128]{0,2,1:T(8,128)(2,1)S(1)}, u32[]{:S(2)}, u32[]{:S(2)}) async-start(bf16[128,16,128]{0,2,1:T(8,128)(2,1)} %bitcast.19), calls=%async_computation.1 | async-start | bytes 1048576 | tf_op jit(solution)/shard_map/all_to_all | solution.py:18
Sparse Core Ops, SparseCore 0:
  37.1 62.3 all-gather.2
  101.3 55.4 all-gather.4
where the time goes:
time: 577 us; the launch traced here: 572 us
  local copies, waits for them, and re-layouts  288 us (50%)
  waiting for transfers between devices  82.6 us (14%)
  blocking collectives  77.2 us (13%)
  matrix products  71 us (12%)
  loops' own time  21.9 us (4%)
  between operations  13.6 us (2%)
  other arithmetic  13.1 us (2%)
    gather x96, local copies, waits for them, and re-layouts, pick_tile(): return tiles[column]  258 us
    all_gather x1, waiting for transfers between devices, per_device(): value_piece = lax.all_gather(value_group, 'blk', axis=0, tiled=True)  57.4 us
    dot_general x32, matrix products, one_slot(): jnp.einsum('hgqd,hgkd->hgqk', query_blocks, keys_now, preferred_element_t...  44 us
    all_to_all x1, blocking collectives, per_device(): lax.all_to_all(keys, 'head', split_axis=1, concat_axis=0, tiled=True)  28.7 us
    dot_general x32, matrix products, one_slot(): jnp.einsum('hgqk,hgkd->hgqd', weights.astype(jnp.bfloat16), current_value...  26.9 us
    all_to_all x1, blocking collectives, per_device(): lax.all_to_all(output, 'head', split_axis=0, concat_axis=1, tiled=True)  26.7 us
    another operation x1, loops' own time, per_device(): run_max, run_sum, run_acc = lax.fori_loop(0, hits, one_slot, start_carry)  21.9 us
    all_to_all x1, blocking collectives, per_device(): lax.all_to_all(values, 'head', split_axis=1, concat_axis=0, tiled=True)  21.8 us
  transfers between devices with their start and end apart: 3, of which 3 were waited for; matrix products, arithmetic and copies ran while one was open for 2% of the time, Pallas kernels for 0%

commit v1 on v0

v1 whole, which is shorter than its diff:
```python
import functools
import math

import jax
import jax.numpy as jnp
from jax import lax
from jax.experimental import pallas as pl
from jax.experimental.pallas import tpu as pltpu
from jax.sharding import PartitionSpec as P

HD = 128
HEADS = 16
BLOCK = 128
SCALE2 = HD**-0.5 * math.log2(math.e)


def attend(width, lists, query, key, value, frame_col, frame_row, out, scores):
    row = pl.program_id(0)
    q = query[...]
    mine = jnp.broadcast_to(frame_col[...], (BLOCK, BLOCK))
    top = None
    for slot in range(width):
        column = lists[row, slot]
        raw = lax.dot_general(q, key[column], (((1,), (1,)), ((), ())), preferred_element_type=jnp.float32)
        now = raw * SCALE2 - jnp.abs(mine - frame_row[column])
        scores[:, slot * BLOCK : (slot + 1) * BLOCK] = now
        top = now if top is None else jnp.maximum(top, now)
    top = jnp.broadcast_to(jnp.max(top, axis=1, keepdims=True), (BLOCK, BLOCK))
    total = jnp.zeros((BLOCK, BLOCK), jnp.float32)
    acc = jnp.zeros((BLOCK, HD), jnp.float32)
    for slot in range(0, width, 2):
        pair = []
        for part in (slot, slot + 1):
            w = jnp.exp2(scores[:, part * BLOCK : (part + 1) * BLOCK] - top)
            total = total + w
            pair.append(w.astype(jnp.bfloat16))
        both = jnp.concatenate([value[lists[row, slot]], value[lists[row, slot + 1]]], axis=0)
        acc = acc + jnp.dot(jnp.concatenate(pair, axis=1), both, preferred_element_type=jnp.float32)
    out[...] = (acc / jnp.sum(total, axis=1, keepdims=True)).astype(out.dtype)


def per_device(queries, keys, values, slopes, frames, block_list):
    query_group, key_group, value_group = (
        lax.all_to_all(a, "head", split_axis=1, concat_axis=0, tiled=True) for a in (queries, keys, values)
    )
    group_rows = query_group.shape[0]
    group_blocks = group_rows // BLOCK
    blocks = frames.shape[0] // BLOCK
    width = block_list.shape[2]
    start = lax.axis_index("blk") * group_blocks
    head = lax.axis_index("head")
    slope = lax.dynamic_slice_in_dim(slopes, head, 1) * math.log2(math.e)
    lists = lax.dynamic_slice(block_list, (head, start, 0), (1, group_blocks, width))[0]
    scaled = frames.astype(jnp.float32) * slope
    mine = lax.dynamic_slice_in_dim(scaled, start * BLOCK, group_rows).reshape(group_rows, 1)
    key_all = lax.all_gather(key_group, "blk", axis=0, tiled=True).reshape(blocks, BLOCK, HD)
    value_all = lax.all_gather(value_group, "blk", axis=0, tiled=True).reshape(blocks, BLOCK, HD)
    output = pl.pallas_call(
        functools.partial(attend, width),
        out_shape=jax.ShapeDtypeStruct((group_rows, HD), jnp.bfloat16),
        grid_spec=pltpu.PrefetchScalarGridSpec(
            num_scalar_prefetch=1,
            grid=(group_blocks,),
            in_specs=[
                pl.BlockSpec((BLOCK, HD), lambda i, t: (i, 0)),
                pl.BlockSpec((blocks, BLOCK, HD), lambda i, t: (0, 0, 0), pipeline_mode=pl.Buffered(1)),
                pl.BlockSpec((blocks, BLOCK, HD), lambda i, t: (0, 0, 0), pipeline_mode=pl.Buffered(1)),
                pl.BlockSpec((BLOCK, 1), lambda i, t: (i, 0)),
                pl.BlockSpec((blocks, 1, BLOCK), lambda i, t: (0, 0, 0), pipeline_mode=pl.Buffered(1)),
            ],
            out_specs=pl.BlockSpec((BLOCK, HD), lambda i, t: (i, 0)),
            scratch_shapes=[pltpu.VMEM((BLOCK, width * BLOCK), jnp.float32)],
        ),
        compiler_params=pltpu.CompilerParams(vmem_limit_bytes=48 << 20),
    )(lists, query_group, key_all, value_all, mine, scaled.reshape(blocks, 1, BLOCK))
    return lax.all_to_all(output, "head", split_axis=0, concat_axis=1, tiled=True)


def solution(mesh):
    rows = P(("blk", "head"), None)
    return jax.shard_map(
        per_device, mesh=mesh, in_specs=(rows, rows, rows, P(), P(), P()), out_specs=rows, check_vma=False
    )
```

time: 577 us -> 224 us (0.39)
  local copies, waits for them, and re-layouts: 288 us -> 6.94 us
  matrix products: 71 us -> 0 us
  Pallas kernels: 0 us -> 31.4 us
  loops' own time: 21.9 us -> 0 us
  other arithmetic: 13.1 us -> 0.01 us
    gather x133 -> x0, local copies, waits for them, and re-layouts: 280 us -> none  [the longest x96 258 us: pick_tile(): return tiles[column]]
    dot_general x64 -> x0, matrix products: 71 us -> none  [the longest x32 44 us: one_slot(): jnp.einsum('hgqd,hgkd->hgqk', query_blocks, keys_now, preferred_element_t...]
    pallas_call x0 -> x1, Pallas kernels: none -> 31.4 us  [per_device(): pl.pallas_call(functools.partial(attend, width), out_shape=jax.ShapeDtype...]
    another operation x1 -> x0, loops' own time: 21.9 us -> none  [per_device(): run_max, run_sum, run_acc = lax.fori_loop(0, hits, one_slot, start_carry)]
    reduce_sum x33 -> x0, other arithmetic: 6.98 us -> none  [the longest x32 6.96 us: one_slot(): run_sum = run_sum * shrink + jnp.sum(weights, axis=3)]
where the time goes in v1:
time: 224 us; the launch traced here: 223 us
  waiting for transfers between devices  88.1 us (39%)
  blocking collectives  77.1 us (34%)
  Pallas kernels  31.4 us (14%)
  between operations  14.1 us (6%)
  local copies, waits for them, and re-layouts  6.94 us (3%)
  starting transfers between devices  4.87 us (2%)
    all_gather x1, waiting for transfers between devices, per_device(): lax.all_gather(value_group, 'blk', axis=0, tiled=True)  57.4 us
    all_to_all x2, blocking collectives, per_device(): lax.all_to_all(a, 'head', split_axis=1, concat_axis=0, tiled=True)  50.4 us
    pallas_call x1, Pallas kernels, per_device(): pl.pallas_call(functools.partial(attend, width), out_shape=jax.ShapeDtype...  31.4 us
    all_to_all x1, blocking collectives, per_device(): lax.all_to_all(output, 'head', split_axis=0, concat_axis=1, tiled=True)  26.7 us
    all_gather x1, waiting for transfers between devices, per_device(): lax.all_gather(key_group, 'blk', axis=0, tiled=True)  16.1 us
    all_to_all x1, waiting for transfers between devices, per_device(): lax.all_to_all(a, 'head', split_axis=1, concat_axis=0, tiled=True)  14.6 us
    all_to_all x1, starting transfers between devices, per_device(): lax.all_to_all(a, 'head', split_axis=1, concat_axis=0, tiled=True)  4.83 us
  transfers between devices with their start and end apart: 3, of which 3 were waited for; matrix products, arithmetic and copies ran while one was open for 2% of the time, Pallas kernels for 0%

profile of v1, /device:TPU:1, one launch (start us, length us, event | category | flops | bytes accessed | tf_op | source)
XLA Modules:
  0.0 222.6 jit_solution(8253916814554526473)
XLA Ops:
  6.5 0.0 copy-start
  6.5 0.0 all-gather.3.cloned.1.call-start
  6.5 1.4 copy.24
  7.9 0.3 copy.25
  8.2 28.6 %all_to_all.76 = bf16[128,16,128]{2,0,1:T(8,128)(2,1)} all-to-all(bf16[128,16,128]{2,0,1:T(8,128)(2,1)S(1)} %copy.25), channel_id=1, replica_groups=mesh['blk'=16,'head'=16] {'head'}, dimensions={1} | all-to-all | bytes 1048576 | tf_op jit(solution)/shard_map/all_to_all | solution.py:44
  36.8 0.0 all-gather.3.cloned.1.call-update
  36.9 0.0 all-gather.5.cloned.1.call-start
  36.9 1.3 copy.26
  38.2 0.3 copy.27
  38.5 21.8 %all_to_all.77 = bf16[128,16,128]{2,0,1:T(8,128)(2,1)} all-to-all(bf16[128,16,128]{2,0,1:T(8,128)(2,1)S(1)} %copy.27), channel_id=1, replica_groups=mesh['blk'=16,'head'=16] {'head'}, dimensions={1} | all-to-all | bytes 1048576 | tf_op jit(solution)/shard_map/all_to_all | solution.py:44
  60.3 0.0 all-gather.5.cloned.1.call-update
  60.3 0.0 copy-done
  60.3 0.9 copy_bitcast_fusion.1
  61.3 4.8 %all-to-all-start = ((bf16[128,16,128]{2,0,1:T(8,128)(2,1)}), bf16[128,16,128]{2,0,1:T(8,128)(2,1)S(1)}, u32[]{:S(2)}, u32[]{:S(2)}) async-start(bf16[128,16,128]{2,0,1:T(8,128)(2,1)} %copy_bitcast_fusion.1), calls=%async_computation | async-start | bytes 1048576 | tf_op jit(solution)/shard_map/all_to_all | solution.py:44
  66.1 0.6 dynamic_slice.10
  66.8 0.8 constant_dynamic-slice_fusion
  67.6 0.1 copy.22
  68.3 0.4 copy.28.frame_col
  68.7 14.6 %all-to-all-done = bf16[128,16,128]{2,0,1:T(8,128)(2,1)S(1)} async-done(((bf16[128,16,128]{2,0,1:T(8,128)(2,1)}), bf16[128,16,128]{2,0,1:T(8,128)(2,1)S(1)}, u32[]{:S(2)}, u32[]{:S(2)}) %all-to-all-start) | async-done | bytes 524320 | tf_op jit(solution)/shard_map/all_to_all | solution.py:44
  83.3 16.1 %all-gather.3.cloned.1.call-done = bf16[32768,128]{1,0:T(8,128)(2,1)} async-done(((bf16[2048,128]{1,0:T(8,128)(2,1)}), bf16[32768,128]{1,0:T(8,128)(2,1)}) %all-gather.3.cloned.1.call-update) | async-done | bytes 8388624 | tf_op jit(solution)/shard_map/all_gather | solution.py:56
  99.4 57.4 %all-gather.5.cloned.1.call-done = bf16[32768,128]{1,0:T(8,128)(2,1)} async-done(((bf16[2048,128]{1,0:T(8,128)(2,1)}), bf16[32768,128]{1,0:T(8,128)(2,1)}) %all-gather.5.cloned.1.call-update) | async-done | bytes 8388624 | tf_op jit(solution)/shard_map/all_gather | solution.py:57
  156.7 31.4 %shard_map.64 = bf16[2048,128]{1,0:T(8,128)(2,1)S(1)} custom-call(s32[16,32]{1,0:T(8,128)S(1)} %bitcast.32, bf16[2048,128]{1,0:T(8,128)(2,1)S(1)} %bitcast.29, bf16[256,128,128]{2,1,0:T(8,128)(2,1)} %bitcast.33, bf16[256,128,128]{2,1,0:T(8,128)(2,1)} %bitcast.34, f32[2048,1]{1,0:T(8,128)S(1)} %copy.28.frame_col, f32[256,1,128]{2,1,0:T(1,128)S(1)} %bitcast.31), custom_call_target="tpu_custom_call" | custom-call | tf_op jit(solution)/shard_map/pallas_call | solution.py:58
  188.2 26.7 %all_to_all.78 = bf16[16,128,128]{2,1,0:T(8,128)(2,1)S(1)} all-to-all(bf16[16,128,128]{2,1,0:T(8,128)(2,1)S(1)} %bitcast.30), channel_id=1, replica_groups=mesh['blk'=16,'head'=16] {'head'}, dimensions={0} | all-to-all | bytes 1048576 | tf_op jit(solution)/shard_map/all_to_all | solution.py:76
  214.9 0.9 copy_bitcast_fusion
  (6 shorter events, 0.0 us)
Async XLA Ops:
  6.5 53.8 %copy-start = (bf16[128,2048]{1,0:T(8,128)(2,1)S(1)}, bf16[128,2048]{1,0:T(8,128)(2,1)}, u32[]{:S(2)}) copy-start(bf16[128,2048]{1,0:T(8,128)(2,1)} %param.6) | copy-start | bytes 1572868
  6.5 59.6 %copy-start.2 = (f32[16]{0:T(128)S(1)}, f32[16]{0:T(128)}, u32[]{:S(2)}) copy-start(f32[16]{0:T(128)} %param.9) | copy-start | bytes 196
  6.5 61.7 %copy-start.1 = (s32[32768]{0:T(1024)S(1)}, s32[32768]{0:T(1024)}, u32[]{:S(2)}) copy-start(s32[32768]{0:T(1024)} %param.10) | copy-start | bytes 393220
  6.5 92.8 %all-gather.3.cloned.1.call-start = ((), (), s32[]{:S(2)}) async-start(), calls=%async_computation.4 | async-start | bytes 8912896 | tf_op jit(solution)/shard_map/all_gather | solution.py:56
  36.9 119.9 %all-gather.5.cloned.1.call-start = ((), (), s32[]{:S(2)}) async-start(), calls=%async_computation.5 | async-start | bytes 8912896 | tf_op jit(solution)/shard_map/all_gather | solution.py:57
  61.3 22.0 %all-to-all-start = ((bf16[128,16,128]{2,0,1:T(8,128)(2,1)}), bf16[128,16,128]{2,0,1:T(8,128)(2,1)S(1)}, u32[]{:S(2)}, u32[]{:S(2)}) async-start(bf16[128,16,128]{2,0,1:T(8,128)(2,1)} %copy_bitcast_fusion.1), calls=%async_computation | async-start | bytes 1048576 | tf_op jit(solution)/shard_map/all_to_all | solution.py:44
Sparse Core Ops, SparseCore 0:
  37.0 62.3 all-gather.2
  101.2 55.4 all-gather.4

commit v2 on v1

v2 whole, which is shorter than its diff:
```python
import functools
import math

import jax
import jax.numpy as jnp
from jax import lax
from jax.experimental import pallas as pl
from jax.experimental.pallas import tpu as pltpu
from jax.sharding import PartitionSpec as P

HD = 128
BLOCK = 128
LOG2E = math.log2(math.e)
SCALE2 = HD**-0.5 * LOG2E
Z = 8
PLANE = 16
TILES = 16
CHUNK = 4
MESH = pl.DeviceIdType.MESH


def offset_at(p):
    step = (p + 1) // 2
    return (Z + step * (2 * (p % 2) - 1)) % Z


PLACES = [0, 1, 3, 5, 7, 6, 4, 2]


def kernel(width, lists, rows, q_hbm, k_hbm, v_hbm, frame_col, frame_row, out,
           q_all, k_all, v_all, o_all, scores,
           local, send, scat, x_a, x_b, y_up, y_down, y_far, core_in, q_in, o_send, o_in):
    blk, head = lax.axis_index("blk"), lax.axis_index("head")
    z, xh = head // 2, head % 2
    xl, core = (blk // 2) % 2, blk % 2
    xp = blk + 2 - 4 * xl
    cp = blk + 1 - 2 * core
    yu, yd, yo = (blk + 4) % PLANE, (blk + 12) % PLANE, (blk + 8) % PLANE
    xpu, xpd, xpo = (xp + 4) % PLANE, (xp + 12) % PLANE, (xp + 8) % PLANE

    def peer(e, dz):
        return (xp if e else blk, ((z + dz) % Z) * 2 + (1 - xh if e else xh))

    peers = [peer(e, dz) for e in (0, 1) for dz in range(Z) if (e, dz) != (0, 0)]
    near = [(xp, head), (cp, head), (yu, head), (yd, head)]
    barrier = pltpu.get_barrier_semaphore()
    for d in peers + near:
        pl.semaphore_signal(barrier, inc=1, device_id=d, device_id_type=MESH)
    pl.semaphore_wait(barrier, len(peers) + len(near))

    def head_tile(ref, h):
        return ref.at[:, pl.ds(pl.multiple_of(h * HD, HD), HD)]

    def scatter(ref, dst, base_of, sem_of):
        for half in (0, 1):
            for e in (0, 1):
                for p in range(half * CHUNK, (half + 1) * CHUNK):
                    dz = (Z - offset_at(p)) % Z
                    if (e, dz) == (0, 0):
                        continue
                    to = peer(e, dz)
                    pltpu.make_async_remote_copy(
                        head_tile(ref, to[1]), dst.at[base_of(to[0]) + e * Z + p],
                        sem_of(None), sem_of(2 * half + e), device_id=to, device_id_type=MESH,
                    ).start()

    mine = blk * TILES
    own = [
        pltpu.make_async_copy(head_tile(ref, head), dst, local.at[n])
        for n, (ref, dst) in enumerate(((k_hbm, k_all.at[mine]), (v_hbm, v_all.at[mine]), (q_hbm, q_all.at[0])))
    ]
    for c in own:
        c.start()
    scatter(k_hbm, k_all, lambda b: b * TILES, lambda n: send.at[0] if n is None else scat.at[n])
    scatter(q_hbm, q_all, lambda b: 0, lambda n: send.at[2] if n is None else q_in.at[0])
    scatter(v_hbm, v_all, lambda b: b * TILES, lambda n: send.at[1] if n is None else scat.at[4 + n])

    def take(ref, start, tiles, sem):
        view = ref.at[pl.ds(start, tiles)]
        pltpu.make_async_copy(view, view, sem).wait()

    def gather(t, ref):
        def at(origin, ck):
            half, e = divmod(ck, 2)
            return origin * TILES + e * Z + half * CHUNK

        def push(start, tiles, to, sem):
            view = ref.at[pl.ds(start, tiles)]
            pltpu.make_async_remote_copy(
                view, view, send.at[t], sem, device_id=(to, head), device_id_type=MESH
            ).start()

        def to_core(start):
            push(start, CHUNK, cp, core_in.at[t])

        def begin(ck):
            s = at(blk, ck)
            if ck == 0:
                own[t].wait()
                take(ref, s + 1, CHUNK - 1, scat.at[4 * t + ck])
            else:
                take(ref, s, CHUNK, scat.at[4 * t + ck])
            first = ck % 2 == 0
            push(s, CHUNK, xp, x_a.at[2 * t + ck // 2] if first else x_b.at[8 * t + ck // 2 * 4])
            push(s, CHUNK, yu, y_up.at[6 * t + ck])
            push(s, CHUNK, yd, y_down.at[6 * t + ck])
            to_core(s)

        def across(ck):
            s = at(xp, ck)
            take(ref, s, CHUNK, x_a.at[2 * t + ck // 2])
            push(s, CHUNK, yu, y_up.at[6 * t + 4 + ck // 2])
            push(s, CHUNK, yd, y_down.at[6 * t + 4 + ck // 2])
            to_core(s)

        def along(ck, partner):
            n = 6 * t + (4 + ck // 2 if partner else ck)
            h = CHUNK // 2
            s = at(xpd if partner else yd, ck)
            take(ref, s, CHUNK, y_up.at[n])
            push(s, h, yu, y_far.at[n])
            if ck % 2:
                push(s, CHUNK, xp, x_b.at[8 * t + ck // 2 * 4 + 1])
            to_core(s)
            s = at(xpu if partner else yu, ck)
            take(ref, s, CHUNK, y_down.at[n])
            push(s + h, h, yd, y_far.at[n])
            if ck % 2:
                push(s, CHUNK, xp, x_b.at[8 * t + ck // 2 * 4 + 2])
            to_core(s)

        def far(ck, partner):
            n = 6 * t + (4 + ck // 2 if partner else ck)
            s = at(xpo if partner else yo, ck)
            take(ref, s, CHUNK, y_far.at[n])
            if ck % 2:
                push(s, CHUNK, xp, x_b.at[8 * t + ck // 2 * 4 + 3])
            to_core(s)

        def beside(ck, n):
            s = at((xp, xpd, xpu, xpo)[n], ck)
            take(ref, s, CHUNK, x_b.at[8 * t + ck // 2 * 4 + n])
            to_core(s)

        def finish():
            take(ref, 0, TILES * PLANE // 2, core_in.at[t])

        return [
            lambda: begin(0),
            lambda: begin(1),
            lambda: across(0),
            lambda: along(0, False),
            lambda: begin(2),
            lambda: along(1, False),
            lambda: beside(1, 0),
            lambda: along(0, True),
            lambda: begin(3),
            lambda: across(2),
            lambda: far(0, False),
            lambda: far(1, False),
            lambda: along(2, False),
            lambda: beside(1, 1),
            lambda: beside(1, 2),
            lambda: far(0, True),
            lambda: along(3, False),
            lambda: beside(3, 0),
            lambda: along(2, True),
            lambda: beside(1, 3),
            lambda: far(2, False),
            lambda: far(3, False),
            lambda: beside(3, 1),
            lambda: beside(3, 2),
            lambda: far(2, True),
            lambda: beside(3, 3),
            finish,
        ]

    for step in gather(0, k_all) + gather(1, v_all):
        step()
    own[2].wait()
    take(q_all, 1, TILES - 1, q_in.at[0])

    def home(i):
        e, dz = i // Z, offset_at(i % Z)
        to = ((z + dz) % Z) * 2 + (xh + e) % 2
        return (blk + e * (2 - 4 * xl), to)

    def block_row(j, carry):
        i = TILES - 1 - j
        q = q_all[i]
        here = jnp.broadcast_to(frame_col[pl.ds(pl.multiple_of(i * BLOCK, BLOCK), BLOCK), :], (BLOCK, BLOCK))
        top = None
        for slot in range(width):
            raw = lax.dot_general(
                q, k_all[lists[i, slot]], (((1,), (1,)), ((), ())), preferred_element_type=jnp.float32
            )
            now = raw * SCALE2 - jnp.abs(here - frame_row[rows[i, slot]])
            scores[:, slot * BLOCK : (slot + 1) * BLOCK] = now
            top = now if top is None else jnp.maximum(top, now)
        top = jnp.broadcast_to(jnp.max(top, axis=1, keepdims=True), (BLOCK, BLOCK))
        total = jnp.zeros((BLOCK, BLOCK), jnp.float32)
        acc = jnp.zeros((BLOCK, HD), jnp.float32)
        for slot in range(0, width, 2):
            pair = []
            for part in (slot, slot + 1):
                w = jnp.exp2(scores[:, part * BLOCK : (part + 1) * BLOCK] - top)
                total = total + w
                pair.append(w.astype(jnp.bfloat16))
            both = jnp.concatenate([v_all[lists[i, slot]], v_all[lists[i, slot + 1]]], axis=0)
            acc = acc + jnp.dot(jnp.concatenate(pair, axis=1), both, preferred_element_type=jnp.float32)
        o_all[i] = (acc / jnp.sum(total, axis=1, keepdims=True)).astype(o_all.dtype)

        @pl.when(i > 0)
        def _():
            pltpu.make_async_remote_copy(
                o_all.at[i], head_tile(out, head), o_send.at[0], o_in.at[0], device_id=home(i), device_id_type=MESH
            ).start()

        return carry

    lax.fori_loop(0, TILES, block_row, 0)
    last = pltpu.make_async_copy(o_all.at[0], head_tile(out, head), local.at[3])
    last.start()
    last.wait()
    take(o_all, 1, TILES - 1, o_in.at[0])
    take(o_all, 1, TILES - 1, o_send.at[0])
    take(q_all, 1, TILES - 1, send.at[2])
    for t, ref in ((0, k_all), (1, v_all)):
        take(ref, 0, 15 + 128 + 40 + 72, send.at[t])


def per_device(queries, keys, values, slopes, frames, block_list):
    width = block_list.shape[2]
    blocks = frames.shape[0] // BLOCK
    blk, head = lax.axis_index("blk"), lax.axis_index("head")
    z, xh = head // 2, head % 2
    slope = lax.dynamic_slice_in_dim(slopes, head, 1) * LOG2E
    scaled = frames.astype(jnp.float32) * slope

    def mine(array):
        parts = array.reshape(PLANE, Z, 2, -1)
        sources = (z + jnp.array([offset_at(p) for p in range(Z)])) % Z
        return jnp.concatenate(
            [
                lax.dynamic_slice(parts, (b, 0, x, 0), (1, Z, 1, parts.shape[3]))[0, :, 0][sources]
                for b, x in ((blk, xh), (blk ^ 2, 1 - xh))
            ]
        )

    rows = mine(lax.dynamic_index_in_dim(block_list, head, 0, keepdims=False))
    source_blk, source_z, source_x = rows // TILES, rows % TILES // 2, rows % 2
    column = source_x ^ xh
    place = jnp.array(PLACES)[(source_z - z) % Z]
    lists = (source_blk ^ (2 * column)) * TILES + column * Z + place
    frame_col = mine(scaled.reshape(blocks, BLOCK)).reshape(TILES * BLOCK, 1)
    frame_row = scaled.reshape(blocks, 1, BLOCK)
    smem, vmem = pl.BlockSpec(memory_space=pltpu.SMEM), pl.BlockSpec(memory_space=pltpu.VMEM)
    hbm = pl.BlockSpec(memory_space=pl.ANY)
    dma = pltpu.SemaphoreType.DMA
    return pl.pallas_call(
        functools.partial(kernel, width),
        out_shape=jax.ShapeDtypeStruct(queries.shape, jnp.bfloat16),
        in_specs=[smem, smem, hbm, hbm, hbm, vmem, vmem],
        out_specs=hbm,
        scratch_shapes=[
            pltpu.VMEM((TILES, BLOCK, HD), jnp.bfloat16),
            pltpu.VMEM((blocks, BLOCK, HD), jnp.bfloat16),
            pltpu.VMEM((blocks, BLOCK, HD), jnp.bfloat16),
            pltpu.VMEM((TILES, BLOCK, HD), jnp.bfloat16),
            pltpu.VMEM((BLOCK, width * BLOCK), jnp.float32),
            dma((4,)), dma((3,)), dma((8,)), dma((4,)), dma((16,)), dma((12,)), dma((12,)), dma((12,)),
            dma((2,)), dma((1,)), dma((1,)), dma((1,)),
        ],
        compiler_params=pltpu.CompilerParams(collective_id=0, has_side_effects=True, vmem_limit_bytes=56 << 20),
    )(lists, rows, queries, keys, values, frame_col, frame_row)


def solution(mesh):
    rows = P(("blk", "head"), None)
    return jax.shard_map(
        per_device, mesh=mesh, in_specs=(rows, rows, rows, P(), P(), P()), out_specs=rows, check_vma=False
    )
```

time: 224 us -> 122 us (0.54)
  waiting for transfers between devices: 88.1 us -> 0 us
  Pallas kernels: 31.4 us -> 109 us
  blocking collectives: 77.1 us -> 0 us
  between operations: 14.1 us -> 0.76 us
  starting transfers between devices: 4.87 us -> 0 us
  local copies, waits for them, and re-layouts: 6.94 us -> 11.7 us
    all_to_all x3 -> x0, blocking collectives: 77.1 us -> none  [the longest x2 50.4 us: per_device(): lax.all_to_all(a, 'head', split_axis=1, concat_axis=0, tiled=True)]
    pallas_call x1, Pallas kernels: 31.4 us -> 109 us  [per_device(): pl.pallas_call(functools.partial(kernel, width), out_shape=jax.ShapeDtype...]
    all_gather x2 -> x0, waiting for transfers between devices: 73.4 us -> none  [the longest x1 57.4 us: per_device(): lax.all_gather(value_group, 'blk', axis=0, tiled=True)]
    all_to_all x1 -> x0, waiting for transfers between devices: 14.6 us -> none  [per_device(): lax.all_to_all(a, 'head', split_axis=1, concat_axis=0, tiled=True)]
    gather x0 -> x6, local copies, waits for them, and re-layouts: none -> 5.64 us  [the longest x2 3.42 us: per_device(): place = jnp.array(PLACES)[(source_z - z) % Z]]
    all_to_all x1 -> x0, starting transfers between devices: 4.83 us -> none  [per_device(): lax.all_to_all(a, 'head', split_axis=1, concat_axis=0, tiled=True)]
    all_to_all x4 -> x0, local copies, waits for them, and re-layouts: 2.37 us -> none  [the longest x3 1.5 us: per_device(): lax.all_to_all(a, 'head', split_axis=1, concat_axis=0, tiled=True)]
  transfers between devices with their start and end apart: 3 -> 0, of which waited for: 3 -> 0; matrix products, arithmetic and copies ran while one was open for 2% -> 0% of each run, Pallas kernels for 0% -> 0%
where the time goes in v2:
time: 122 us
  Pallas kernels  109 us (89%)
  local copies, waits for them, and re-layouts  11.7 us (10%)
    pallas_call x1, Pallas kernels, per_device(): pl.pallas_call(functools.partial(kernel, width), out_shape=jax.ShapeDtype...  109 us
    unnamed x17, local copies, waits for them, and re-layouts  4.01 us
    gather x2, local copies, waits for them, and re-layouts, per_device(): place = jnp.array(PLACES)[(source_z - z) % Z]  3.42 us

profile of v2, /device:TPU:1, one launch (start us, length us, event | category | flops | bytes accessed | tf_op | source)
XLA Modules:
  0.0 121.6 jit_solution(1630936540816215017)
XLA Ops:
  0.0 0.0 copy-start
  0.0 0.0 copy-start.5
  0.0 0.7 copy-done.5
  0.7 0.6 dynamic_slice.22
  2.0 0.0 copy-start.6
  2.0 0.6 copy-done.6
  2.6 0.0 copy-done
  2.7 0.1 copy.12
  2.8 0.6 gather_fusion
  3.3 0.6 gather_fusion.1
  3.9 0.1 reshape.228
  4.0 0.6 copy-done.1
  4.7 3.3 %gather_fusion.2 = s32[512]{0:T(512)S(1)} fusion(s32[8]{0:T(128)S(1)} %copy-done.1, s32[1024]{0:T(1024)S(1)} %pad_clamp_fusion), kind=kCustom, calls=%fused_computation.2 | custom fusion | bytes 6144 | tf_op jit(solution)/shard_map/gather | solution.py:253
  8.0 0.1 reshape.227
  8.1 0.6 fusion.4.lists
  8.7 0.0 copy-done.4
  8.7 0.0 copy-done.3
  8.7 0.0 copy-start.2
  8.8 0.6 gather_fusion.3
  9.3 0.6 gather_fusion.4
  9.9 1.3 %copy.11.frame_col = f32[2048,1]{1,0:T(8,128)} copy(f32[2048,1]{0,1:T(1,128)S(1)} %bitcast.22) | data formatting | bytes 16384 | tf_op jit(solution)/shard_map/reshape | solution.py:255
  11.3 0.0 copy-done.2
  11.3 108.5 %shard_map.91 = bf16[128,2048]{1,0:T(8,128)(2,1)} custom-call(s32[16,32]{1,0:T(8,128)} %fusion.4.lists, s32[16,32]{1,0:T(8,128)} %copy-done.4, bf16[128,2048]{1,0:T(8,128)(2,1)} %q_hbm.1, bf16[128,2048]{1,0:T(8,128)(2,1)} %k_hbm.1, bf16[128,2048]{1,0:T(8,128)(2,1)} %v_hbm.1, f32[2048,1]{1,0:T(8,128)} %copy.11.frame_col, f32[256,1,128]{2,1,0:T(1,128)} %bitcast.14), custom_call_target="tpu_custom_call" | custom-call | tf_op jit(solution)/shard_map/pallas_call | solution.py:260
  119.8 1.9 %copy.15 = bf16[128,2048]{1,0:T(8,128)(2,1)} copy(bf16[128,2048]{1,0:T(8,128)(2,1)} %shard_map.91) | data formatting | bytes 1048576
  (14 shorter events, 0.1 us)
Async XLA Ops:
  0.0 2.6 %copy-start = (s32[16,256,32]{1,2,0:T(8,128)S(1)}, s32[16,256,32]{1,2,0:T(8,128)}, u32[]{:S(2)}) copy-start(s32[16,256,32]{1,2,0:T(8,128)} %param.14) | copy-start | bytes 1572868
  0.0 0.7 copy-start.5
  2.0 0.7 copy-start.6
  4.0 0.7 copy-start.1
  4.7 4.1 %copy-start.3 = (s32[32768]{0:T(1024)S(1)}, s32[32768]{0:T(1024)}, u32[]{:S(2)}) copy-start(s32[32768]{0:T(1024)} %param.13) | copy-start | bytes 393220
  8.1 0.6 copy-start.4
  8.7 2.5 %copy-start.2 = (f32[32768]{0:T(1024)}, f32[32768]{0:T(1024)S(1)}, u32[]{:S(2)}) copy-start(f32[32768]{0:T(1024)S(1)} %convert_multiply_fusion) | copy-start | bytes 393220

commit v3 on v2

--- a/solution.py
+++ b/solution.py
@@ -24,11 +24,12 @@
     return (Z + step * (2 * (p % 2) - 1)) % Z
 
 
-PLACES = [0, 1, 3, 5, 7, 6, 4, 2]
-
-
-def kernel(width, lists, rows, q_hbm, k_hbm, v_hbm, frame_col, frame_row, out,
-           q_all, k_all, v_all, o_all, scores,
+def place_of(dz):
+    return jnp.where(dz <= Z // 2, jnp.maximum(2 * dz - 1, 0), 2 * (Z - dz))
+
+
+def kernel(width, slopes, list_hbm, q_hbm, k_hbm, v_hbm, frame_hbm, out,
+           rows, tiles_of, frame_row, here_all, q_all, k_all, v_all, o_all, scores, w_all, total_all,
            local, send, scat, x_a, x_b, y_up, y_down, y_far, core_in, q_in, o_send, o_in):
     blk, head = lax.axis_index("blk"), lax.axis_index("head")
     z, xh = head // 2, head % 2
@@ -65,6 +66,14 @@
                     ).start()
 
     mine = blk * TILES
+    heads = rows.shape[1]
+    pattern = [
+        pltpu.make_async_copy(
+            list_hbm.at[head, pl.ds(pl.multiple_of(b * heads, heads), heads)], rows.at[e], local.at[4 + e]
+        )
+        for e, b in ((0, blk), (1, xp))
+    ]
+    frame_copy = pltpu.make_async_copy(frame_hbm, frame_row, local.at[6])
     own = [
         pltpu.make_async_copy(head_tile(ref, head), dst, local.at[n])
         for n, (ref, dst) in enumerate(((k_hbm, k_all.at[mine]), (v_hbm, v_all.at[mine]), (q_hbm, q_all.at[0])))
@@ -74,6 +83,27 @@
     scatter(k_hbm, k_all, lambda b: b * TILES, lambda n: send.at[0] if n is None else scat.at[n])
     scatter(q_hbm, q_all, lambda b: 0, lambda n: send.at[2] if n is None else q_in.at[0])
     scatter(v_hbm, v_all, lambda b: b * TILES, lambda n: send.at[1] if n is None else scat.at[4 + n])
+
+    for c in pattern:
+        c.start()
+    frame_copy.start()
+
+    def source(i):
+        e = i // Z
+        return e, (z + offset_at(i % Z)) % Z * 2 + (xh + e) % 2
+
+    slope = slopes[head] * LOG2E
+    frame_copy.wait()
+    for c in pattern:
+        c.wait()
+
+    def query_frames(i, carry):
+        e, row = source(i)
+        line = frame_row[(blk + e * (2 - 4 * xl)) * heads + row].astype(jnp.float32) * slope
+        here_all[i] = jnp.broadcast_to(line, (BLOCK, BLOCK)).T
+        return carry
+
+    lax.fori_loop(0, TILES, query_frames, 0)
 
     def take(ref, start, tiles, sem):
         view = ref.at[pl.ds(start, tiles)]
@@ -175,10 +205,49 @@
             finish,
         ]
 
-    for step in gather(0, k_all) + gather(1, v_all):
+    def weigh(i):
+        e, row = source(i)
+        q = q_all[i]
+        here = here_all[i]
+        top = None
+        for slot in range(width):
+            block = rows[e, row, slot]
+            column = (block + xh) % 2
+            group, dz = block // heads, (block % heads // 2 - z + Z) % Z
+            tile = (group + column * (2 - group // 2 % 2 * 4)) * TILES + column * Z + place_of(dz)
+            tiles_of[i, slot] = tile
+            raw = lax.dot_general(q, k_all[tile], (((1,), (1,)), ((), ())), preferred_element_type=jnp.float32)
+            now = raw * SCALE2 - jnp.abs(here - frame_row[block].astype(jnp.float32) * slope)
+            scores[:, slot * BLOCK : (slot + 1) * BLOCK] = now
+            top = now if top is None else jnp.maximum(top, now)
+        top = jnp.broadcast_to(jnp.max(top, axis=1, keepdims=True), (BLOCK, BLOCK))
+        total = jnp.zeros((BLOCK, BLOCK), jnp.float32)
+        for slot in range(width):
+            w = jnp.exp2(scores[:, slot * BLOCK : (slot + 1) * BLOCK] - top)
+            total = total + w
+            w_all[i, :, slot * BLOCK : (slot + 1) * BLOCK] = w.astype(w_all.dtype)
+        total_all[i] = total
+
+    key_steps, value_steps = gather(0, k_all), gather(1, v_all)
+    early = 2
+    for step in key_steps[:-5] + value_steps[:early] + key_steps[-5:]:
         step()
     own[2].wait()
     take(q_all, 1, TILES - 1, q_in.at[0])
+    later = value_steps[early:]
+
+    def weigh_and_pass(i, carry):
+        weigh(i)
+        for n in range(TILES):
+
+            @pl.when(i == n)
+            def _():
+                for step in later[n * len(later) // TILES : (n + 1) * len(later) // TILES]:
+                    step()
+
+        return carry
+
+    lax.fori_loop(0, TILES, weigh_and_pass, 0)
 
     def home(i):
         e, dz = i // Z, offset_at(i % Z)
@@ -187,28 +256,13 @@
 
     def block_row(j, carry):
         i = TILES - 1 - j
-        q = q_all[i]
-        here = jnp.broadcast_to(frame_col[pl.ds(pl.multiple_of(i * BLOCK, BLOCK), BLOCK), :], (BLOCK, BLOCK))
-        top = None
-        for slot in range(width):
-            raw = lax.dot_general(
-                q, k_all[lists[i, slot]], (((1,), (1,)), ((), ())), preferred_element_type=jnp.float32
-            )
-            now = raw * SCALE2 - jnp.abs(here - frame_row[rows[i, slot]])
-            scores[:, slot * BLOCK : (slot + 1) * BLOCK] = now
-            top = now if top is None else jnp.maximum(top, now)
-        top = jnp.broadcast_to(jnp.max(top, axis=1, keepdims=True), (BLOCK, BLOCK))
-        total = jnp.zeros((BLOCK, BLOCK), jnp.float32)
         acc = jnp.zeros((BLOCK, HD), jnp.float32)
         for slot in range(0, width, 2):
-            pair = []
-            for part in (slot, slot + 1):
-                w = jnp.exp2(scores[:, part * BLOCK : (part + 1) * BLOCK] - top)
-                total = total + w
-                pair.append(w.astype(jnp.bfloat16))
-            both = jnp.concatenate([v_all[lists[i, slot]], v_all[lists[i, slot + 1]]], axis=0)
-            acc = acc + jnp.dot(jnp.concatenate(pair, axis=1), both, preferred_element_type=jnp.float32)
-        o_all[i] = (acc / jnp.sum(total, axis=1, keepdims=True)).astype(o_all.dtype)
+            both = jnp.concatenate([v_all[tiles_of[i, slot]], v_all[tiles_of[i, slot + 1]]], axis=0)
+            acc = acc + jnp.dot(
+                w_all[i, :, slot * BLOCK : (slot + 2) * BLOCK], both, preferred_element_type=jnp.float32
+            )
+        o_all[i] = (acc / jnp.sum(total_all[i], axis=1, keepdims=True)).astype(o_all.dtype)
 
         @pl.when(i > 0)
         def _():
@@ -230,49 +284,32 @@
 
 
 def per_device(queries, keys, values, slopes, frames, block_list):
-    width = block_list.shape[2]
-    blocks = frames.shape[0] // BLOCK
-    blk, head = lax.axis_index("blk"), lax.axis_index("head")
-    z, xh = head // 2, head % 2
-    slope = lax.dynamic_slice_in_dim(slopes, head, 1) * LOG2E
-    scaled = frames.astype(jnp.float32) * slope
-
-    def mine(array):
-        parts = array.reshape(PLANE, Z, 2, -1)
-        sources = (z + jnp.array([offset_at(p) for p in range(Z)])) % Z
-        return jnp.concatenate(
-            [
-                lax.dynamic_slice(parts, (b, 0, x, 0), (1, Z, 1, parts.shape[3]))[0, :, 0][sources]
-                for b, x in ((blk, xh), (blk ^ 2, 1 - xh))
-            ]
-        )
-
-    rows = mine(lax.dynamic_index_in_dim(block_list, head, 0, keepdims=False))
-    source_blk, source_z, source_x = rows // TILES, rows % TILES // 2, rows % 2
-    column = source_x ^ xh
-    place = jnp.array(PLACES)[(source_z - z) % Z]
-    lists = (source_blk ^ (2 * column)) * TILES + column * Z + place
-    frame_col = mine(scaled.reshape(blocks, BLOCK)).reshape(TILES * BLOCK, 1)
-    frame_row = scaled.reshape(blocks, 1, BLOCK)
-    smem, vmem = pl.BlockSpec(memory_space=pltpu.SMEM), pl.BlockSpec(memory_space=pltpu.VMEM)
+    heads, blocks, width = block_list.shape
+    smem = pl.BlockSpec(memory_space=pltpu.SMEM)
     hbm = pl.BlockSpec(memory_space=pl.ANY)
     dma = pltpu.SemaphoreType.DMA
     return pl.pallas_call(
         functools.partial(kernel, width),
         out_shape=jax.ShapeDtypeStruct(queries.shape, jnp.bfloat16),
-        in_specs=[smem, smem, hbm, hbm, hbm, vmem, vmem],
+        in_specs=[smem, hbm, hbm, hbm, hbm, hbm],
         out_specs=hbm,
         scratch_shapes=[
+            pltpu.SMEM((2, heads, width), jnp.int32),
+            pltpu.SMEM((TILES, width), jnp.int32),
+            pltpu.VMEM((blocks, 1, BLOCK), jnp.int32),
+            pltpu.VMEM((TILES, BLOCK, BLOCK), jnp.float32),
             pltpu.VMEM((TILES, BLOCK, HD), jnp.bfloat16),
             pltpu.VMEM((blocks, BLOCK, HD), jnp.bfloat16),
             pltpu.VMEM((blocks, BLOCK, HD), jnp.bfloat16),
             pltpu.VMEM((TILES, BLOCK, HD), jnp.bfloat16),
             pltpu.VMEM((BLOCK, width * BLOCK), jnp.float32),
-            dma((4,)), dma((3,)), dma((8,)), dma((4,)), dma((16,)), dma((12,)), dma((12,)), dma((12,)),
+            pltpu.VMEM((TILES, BLOCK, width * BLOCK), jnp.bfloat16),
+            pltpu.VMEM((TILES, BLOCK, BLOCK), jnp.float32),
+            dma((7,)), dma((3,)), dma((8,)), dma((4,)), dma((16,)), dma((12,)), dma((12,)), dma((12,)),
             dma((2,)), dma((1,)), dma((1,)), dma((1,)),
         ],
         compiler_params=pltpu.CompilerParams(collective_id=0, has_side_effects=True, vmem_limit_bytes=56 << 20),
-    )(lists, rows, queries, keys, values, frame_col, frame_row)
+    )(slopes, block_list, queries, keys, values, frames.reshape(blocks, 1, BLOCK))
 
 
 def solution(mesh):

time: 122 us -> 103 us (0.84)
  Pallas kernels: 109 us -> 97.9 us
  local copies, waits for them, and re-layouts: 11.7 us -> 4.88 us
    pallas_call x1, Pallas kernels: 109 us -> 97.9 us  [per_device(): pl.pallas_call(functools.partial(kernel, width), out_shape=jax.ShapeDtype...]
    gather x6 -> x0, local copies, waits for them, and re-layouts: 5.64 us -> none  [the longest x2 3.42 us: per_device(): place = jnp.array(PLACES)[(source_z - z) % Z]]
    reshape x1 -> x0, local copies, waits for them, and re-layouts: 1.34 us -> none  [per_device(): frame_col = mine(scaled.reshape(blocks, BLOCK)).reshape(TILES * BLOCK, 1)]
    unnamed x17 -> x2, local copies, waits for them, and re-layouts: 4.01 us -> 4.88 us
where the time goes in v3:
time: 103 us
  Pallas kernels  97.9 us (95%)
  local copies, waits for them, and re-layouts  4.88 us (5%)
    pallas_call x1, Pallas kernels, per_device(): pl.pallas_call(functools.partial(kernel, width), out_shape=jax.ShapeDtype...  97.9 us
    unnamed x2, local copies, waits for them, and re-layouts  4.88 us

profile of v3, /device:TPU:1, one launch (start us, length us, event | category | flops | bytes accessed | tf_op | source)
XLA Modules:
  0.0 102.8 jit_solution(9801095736391276597)
XLA Ops:
  0.0 3.0 %copy.7.list_hbm = s32[16,256,32]{2,1,0:T(8,128)} copy(s32[16,256,32]{1,2,0:T(8,128)} %param.11) | data formatting | bytes 1048576 | tf_op args[5]
  3.0 97.9 %shard_map.64 = bf16[128,2048]{1,0:T(8,128)(2,1)} custom-call(f32[16]{0:T(128)} %slopes.1, s32[16,256,32]{2,1,0:T(8,128)} %copy.7.list_hbm, bf16[128,2048]{1,0:T(8,128)(2,1)} %q_hbm.1, bf16[128,2048]{1,0:T(8,128)(2,1)} %k_hbm.1, bf16[128,2048]{1,0:T(8,128)(2,1)} %v_hbm.1, s32[256,1,128]{2,1,0:T(1,128)} %bitcast.1), custom_call_target="tpu_custom_call" | custom-call | tf_op jit(solution)/shard_map/pallas_call | solution.py:291
  100.9 1.9 %copy.9 = bf16[128,2048]{1,0:T(8,128)(2,1)} copy(bf16[128,2048]{1,0:T(8,128)(2,1)} %shard_map.64) | data formatting | bytes 1048576

commit v4 on v3

v4 whole, which is shorter than its diff:
```python
import functools
import math

import jax
import jax.numpy as jnp
from jax import lax
from jax.experimental import pallas as pl
from jax.experimental.pallas import tpu as pltpu
from jax.sharding import PartitionSpec as P

HD = 128
BLOCK = 128
LANES = 128
LOG2E = math.log2(math.e)
SCALE2 = HD**-0.5 * LOG2E
Z = 8
PLANE = 16
TILES = 16
CHUNKS = [(0, 4), (9, 3), (4, 5), (12, 4)]
CROSS_FIRST = sum(tiles for _, tiles in CHUNKS[::2])
MESH = pl.DeviceIdType.MESH


def offset_at(p):
    step = (p + 1) // 2
    return (Z + step * (2 * (p % 2) - 1)) % Z


def place_of(dz):
    return jnp.where(dz <= Z // 2, jnp.maximum(2 * dz - 1, 0), 2 * (Z - dz))


def kernel(width, slopes, list_hbm, q_hbm, k_hbm, v_hbm, frame_hbm, out,
           rows, tiles_of, frame_row, here_all, q_all, k_all, v_all, o_all, scores, top_now, w_all, total_all,
           local, send, scat, x_a, x_b, y_up, y_down, y_far, core_in, q_in, o_send, o_in):
    blk, head = lax.axis_index("blk"), lax.axis_index("head")
    z, xh = head // 2, head % 2
    xl, core = (blk // 2) % 2, blk % 2
    xp = blk + 2 - 4 * xl
    cp = blk + 1 - 2 * core
    yu, yd, yo = (blk + 4) % PLANE, (blk + 12) % PLANE, (blk + 8) % PLANE
    xpu, xpd, xpo = (xp + 4) % PLANE, (xp + 12) % PLANE, (xp + 8) % PLANE

    def peer(e, dz):
        return (xp if e else blk, ((z + dz) % Z) * 2 + (1 - xh if e else xh))

    peers = [peer(e, dz) for e in (0, 1) for dz in range(Z) if (e, dz) != (0, 0)]
    near = [(xp, head), (cp, head), (yu, head), (yd, head)]
    barrier = pltpu.get_barrier_semaphore()
    for d in peers + near:
        pl.semaphore_signal(barrier, inc=1, device_id=d, device_id_type=MESH)
    pl.semaphore_wait(barrier, len(peers) + len(near))

    def head_tile(ref, h):
        return ref.at[:, pl.ds(pl.multiple_of(h * HD, HD), HD)]

    def scatter(ref, dst, base_of, sem_of):
        for ck, (first, tiles) in enumerate(CHUNKS):
            for n in range(first, first + tiles):
                e, p = divmod(n, Z)
                dz = (Z - offset_at(p)) % Z
                if (e, dz) == (0, 0):
                    continue
                to = peer(e, dz)
                pltpu.make_async_remote_copy(
                    head_tile(ref, to[1]), dst.at[base_of(to[0]) + n],
                    sem_of(None), sem_of(ck), device_id=to, device_id_type=MESH,
                ).start()

    mine = blk * TILES
    per = LANES // TILES
    pattern = pltpu.make_async_copy(
        list_hbm.at[head, :, pl.ds(pl.multiple_of(blk // per * LANES, LANES), LANES)], rows, local.at[4]
    )
    frame_copy = pltpu.make_async_copy(frame_hbm, frame_row, local.at[5])
    own = [
        pltpu.make_async_copy(head_tile(ref, head), dst, local.at[n])
        for n, (ref, dst) in enumerate(((k_hbm, k_all.at[mine]), (v_hbm, v_all.at[mine]), (q_hbm, q_all.at[0])))
    ]
    for c in own:
        c.start()
    scatter(k_hbm, k_all, lambda b: b * TILES, lambda n: send.at[0] if n is None else scat.at[n])
    scatter(q_hbm, q_all, lambda b: 0, lambda n: send.at[2] if n is None else q_in.at[0])
    scatter(v_hbm, v_all, lambda b: b * TILES, lambda n: send.at[1] if n is None else scat.at[4 + n])

    pattern.start()
    frame_copy.start()

    def source(i):
        e = i // Z
        return e, (z + offset_at(i % Z)) % Z * 2 + (xh + e) % 2

    slope = slopes[head] * LOG2E
    frame_copy.wait()
    pattern.wait()

    def query_frames(i, carry):
        e, row = source(i)
        line = frame_row[(blk + e * (2 - 4 * xl)) * TILES + row].astype(jnp.float32) * slope
        here_all[i] = jnp.broadcast_to(line, (BLOCK, BLOCK)).T
        return carry

    lax.fori_loop(0, TILES, query_frames, 0)

    def take(ref, start, tiles, sem):
        view = ref.at[pl.ds(start, tiles)]
        pltpu.make_async_copy(view, view, sem).wait()

    def gather(t, ref):
        def at(origin, ck):
            return origin * TILES + CHUNKS[ck][0]

        def push(start, tiles, to, sem):
            view = ref.at[pl.ds(start, tiles)]
            pltpu.make_async_remote_copy(
                view, view, send.at[t], sem, device_id=(to, head), device_id_type=MESH
            ).start()

        def to_core(start, ck):
            push(start, CHUNKS[ck][1], cp, core_in.at[t])

        def begin(ck):
            s = at(blk, ck)
            if ck == 0:
                own[t].wait()
                take(ref, s + 1, CHUNKS[ck][1] - 1, scat.at[4 * t + ck])
            else:
                take(ref, s, CHUNKS[ck][1], scat.at[4 * t + ck])
            first = ck % 2 == 0
            push(s, CHUNKS[ck][1], xp, x_a.at[2 * t + ck // 2] if first else x_b.at[8 * t + ck // 2 * 4])
            push(s, CHUNKS[ck][1], yu, y_up.at[6 * t + ck])
            push(s, CHUNKS[ck][1], yd, y_down.at[6 * t + ck])
            to_core(s, ck)

        def across(ck):
            s = at(xp, ck)
            take(ref, s, CHUNKS[ck][1], x_a.at[2 * t + ck // 2])
            push(s, CHUNKS[ck][1], yu, y_up.at[6 * t + 4 + ck // 2])
            push(s, CHUNKS[ck][1], yd, y_down.at[6 * t + 4 + ck // 2])
            to_core(s, ck)

        def along(ck, partner):
            n = 6 * t + (4 + ck // 2 if partner else ck)
            h = (CHUNKS[ck][1] + ck // 2) // 2
            s = at(xpd if partner else yd, ck)
            take(ref, s, CHUNKS[ck][1], y_up.at[n])
            push(s, h, yu, y_far.at[n])
            if ck % 2:
                push(s, CHUNKS[ck][1], xp, x_b.at[8 * t + ck // 2 * 4 + 1])
            to_core(s, ck)
            s = at(xpu if partner else yu, ck)
            take(ref, s, CHUNKS[ck][1], y_down.at[n])
            push(s + h, CHUNKS[ck][1] - h, yd, y_far.at[n])
            if ck % 2:
                push(s, CHUNKS[ck][1], xp, x_b.at[8 * t + ck // 2 * 4 + 2])
            to_core(s, ck)

        def far(ck, partner):
            n = 6 * t + (4 + ck // 2 if partner else ck)
            s = at(xpo if partner else yo, ck)
            take(ref, s, CHUNKS[ck][1], y_far.at[n])
            if ck % 2:
                push(s, CHUNKS[ck][1], xp, x_b.at[8 * t + ck // 2 * 4 + 3])
            to_core(s, ck)

        def beside(ck, n):
            s = at((xp, xpd, xpu, xpo)[n], ck)
            take(ref, s, CHUNKS[ck][1], x_b.at[8 * t + ck // 2 * 4 + n])
            to_core(s, ck)

        def finish():
            take(ref, 0, TILES * PLANE // 2, core_in.at[t])

        return begin, across, along, far, beside, finish

    def score(i):
        e, row = source(i)
        place = (blk + e * (2 - 4 * xl)) % per * TILES + row
        q = q_all[i]
        here = here_all[i]
        top = None
        for slot in range(width):
            block = rows[slot, place]
            column = (block + xh) % 2
            group, dz = block // TILES, (block % TILES // 2 - z + Z) % Z
            tile = (group + column * (2 - group // 2 % 2 * 4)) * TILES + column * Z + place_of(dz)
            tiles_of[i, slot] = tile
            raw = lax.dot_general(q, k_all[tile], (((1,), (1,)), ((), ())), preferred_element_type=jnp.float32)
            now = raw * SCALE2 - jnp.abs(here - frame_row[block].astype(jnp.float32) * slope)
            scores[:, slot * BLOCK : (slot + 1) * BLOCK] = now
            top = now if top is None else jnp.maximum(top, now)
        top_now[...] = jnp.broadcast_to(jnp.max(top, axis=1, keepdims=True), (BLOCK, BLOCK))

    def weigh(i):
        top = top_now[...]
        total = jnp.zeros((BLOCK, BLOCK), jnp.float32)
        for slot in range(width):
            w = jnp.exp2(scores[:, slot * BLOCK : (slot + 1) * BLOCK] - top)
            total = total + w
            w_all[i, :, slot * BLOCK : (slot + 1) * BLOCK] = w.astype(w_all.dtype)
        total_all[i] = total

    begin, across, along, far, beside, finish = gather(0, k_all)
    value_begin, value_across, value_along, value_far, value_beside, value_finish = gather(1, v_all)
    begin(0), begin(1), across(0), along(0, False), begin(2), along(1, False), beside(1, 0), along(0, True)
    begin(3), across(2), far(0, False), far(1, False), along(2, False), beside(1, 1), beside(1, 2), far(0, True)
    along(3, False), beside(3, 0), along(2, True), beside(1, 3), far(2, False), far(3, False)
    value_begin(0), value_begin(1)
    beside(3, 1), beside(3, 2), far(2, True), beside(3, 3), finish()
    own[2].wait()
    take(q_all, 1, TILES - 1, q_in.at[0])
    value_begin(2), value_begin(3)
    later = {
        1: [lambda: value_across(0), lambda: value_along(0, False)],
        3: [lambda: value_along(1, False)],
        5: [lambda: value_beside(1, 0)],
        7: [lambda: value_across(2), lambda: value_along(2, False)],
        10: [lambda: value_along(3, False)],
        12: [lambda: value_beside(3, 0)],
        14: [lambda: value_along(0, True)],
        15: [lambda: value_beside(1, 1)],
        16: [lambda: value_far(0, False)],
        17: [lambda: value_far(1, False)],
        18: [lambda: value_beside(1, 2)],
        20: [lambda: value_along(2, True)],
        21: [lambda: value_beside(3, 1)],
        23: [lambda: value_far(2, False)],
        24: [lambda: value_far(3, False)],
        25: [lambda: value_beside(3, 2)],
        27: [lambda: value_far(0, True)],
        28: [lambda: value_far(2, True)],
        29: [lambda: value_beside(1, 3)],
        31: [lambda: value_beside(3, 3)],
    }

    def pass_on(i, part):
        for half, steps in later.items():
            if half % 2 == part:

                @pl.when(i == half // 2)
                def _(steps=steps):
                    for step in steps:
                        step()

    def weigh_and_pass(i, carry):
        score(i)
        pass_on(i, 0)
        weigh(i)
        pass_on(i, 1)
        return carry

    lax.fori_loop(0, TILES, weigh_and_pass, 0)
    value_finish()

    def home(i):
        e, dz = i // Z, offset_at(i % Z)
        to = ((z + dz) % Z) * 2 + (xh + e) % 2
        return (blk + e * (2 - 4 * xl), to)

    def block_row(j, carry):
        i = TILES - 1 - j
        acc = jnp.zeros((BLOCK, HD), jnp.float32)
        for slot in range(0, width, 2):
            both = jnp.concatenate([v_all[tiles_of[i, slot]], v_all[tiles_of[i, slot + 1]]], axis=0)
            acc = acc + jnp.dot(
                w_all[i, :, slot * BLOCK : (slot + 2) * BLOCK], both, preferred_element_type=jnp.float32
            )
        o_all[i] = (acc / jnp.sum(total_all[i], axis=1, keepdims=True)).astype(o_all.dtype)

        @pl.when(i > 0)
        def _():
            pltpu.make_async_remote_copy(
                o_all.at[i], head_tile(out, head), o_send.at[0], o_in.at[0], device_id=home(i), device_id_type=MESH
            ).start()

        return carry

    lax.fori_loop(0, TILES, block_row, 0)
    last = pltpu.make_async_copy(o_all.at[0], head_tile(out, head), local.at[3])
    last.start()
    last.wait()
    take(o_all, 1, TILES - 1, o_in.at[0])
    take(o_all, 1, TILES - 1, o_send.at[0])
    take(q_all, 1, TILES - 1, send.at[2])
    for t, ref in ((0, k_all), (1, v_all)):
        take(ref, 0, 15 + 128 + (64 - 3 * CROSS_FIRST) + (48 + 3 * CROSS_FIRST), send.at[t])


def per_device(queries, keys, values, slopes, frames, block_list):
    blocks, width = block_list.shape[1:]
    smem = pl.BlockSpec(memory_space=pltpu.SMEM)
    hbm = pl.BlockSpec(memory_space=pl.ANY)
    dma = pltpu.SemaphoreType.DMA
    return pl.pallas_call(
        functools.partial(kernel, width),
        out_shape=jax.ShapeDtypeStruct(queries.shape, jnp.bfloat16),
        in_specs=[smem, hbm, hbm, hbm, hbm, hbm],
        out_specs=hbm,
        scratch_shapes=[
            pltpu.SMEM((width, LANES), jnp.int32),
            pltpu.SMEM((TILES, width), jnp.int32),
            pltpu.VMEM((blocks, 1, BLOCK), jnp.int32),
            pltpu.VMEM((TILES, BLOCK, BLOCK), jnp.float32),
            pltpu.VMEM((TILES, BLOCK, HD), jnp.bfloat16),
            pltpu.VMEM((blocks, BLOCK, HD), jnp.bfloat16),
            pltpu.VMEM((blocks, BLOCK, HD), jnp.bfloat16),
            pltpu.VMEM((TILES, BLOCK, HD), jnp.bfloat16),
            pltpu.VMEM((BLOCK, width * BLOCK), jnp.float32),
            pltpu.VMEM((BLOCK, BLOCK), jnp.float32),
            pltpu.VMEM((TILES, BLOCK, width * BLOCK), jnp.bfloat16),
            pltpu.VMEM((TILES, BLOCK, BLOCK), jnp.float32),
            dma((6,)), dma((3,)), dma((8,)), dma((4,)), dma((16,)), dma((12,)), dma((12,)), dma((12,)),
            dma((2,)), dma((1,)), dma((1,)), dma((1,)),
        ],
        compiler_params=pltpu.CompilerParams(collective_id=0, has_side_effects=True, vmem_limit_bytes=56 << 20),
    )(slopes, block_list.transpose(0, 2, 1), queries, keys, values, frames.reshape(blocks, 1, BLOCK))


def solution(mesh):
    rows = P(("blk", "head"), None)
    return jax.shard_map(
        per_device, mesh=mesh, in_specs=(rows, rows, rows, P(), P(), P()), out_specs=rows, check_vma=False
    )
```

time: 103 us -> 101 us (0.981)
  local copies, waits for them, and re-layouts: 4.88 us -> 1.88 us
    unnamed x2 -> x1, local copies, waits for them, and re-layouts: 4.88 us -> 1.88 us
where the time goes in v4:
time: 101 us
  Pallas kernels  98.9 us (98%)
  local copies, waits for them, and re-layouts  1.88 us (2%)
    pallas_call x1, Pallas kernels, per_device(): pl.pallas_call(functools.partial(kernel, width), out_shape=jax.ShapeDtype...  98.9 us

profile of v4, /device:TPU:1, one launch (start us, length us, event | category | flops | bytes accessed | tf_op | source)
XLA Modules:
  0.0 100.8 jit_solution(8716882213378834635)
XLA Ops:
  0.0 98.9 %shard_map.64 = bf16[128,2048]{1,0:T(8,128)(2,1)} custom-call(f32[16]{0:T(128)} %slopes.1, s32[16,32,256]{2,1,0:T(8,128)} %bitcast.2, bf16[128,2048]{1,0:T(8,128)(2,1)} %q_hbm.1, bf16[128,2048]{1,0:T(8,128)(2,1)} %k_hbm.1, bf16[128,2048]{1,0:T(8,128)(2,1)} %v_hbm.1, s32[256,1,128]{2,1,0:T(1,128)} %bitcast.3), custom_call_target="tpu_custom_call" | custom-call | tf_op jit(solution)/shard_map/pallas_call | solution.py:294
  98.9 1.9 %copy.8 = bf16[128,2048]{1,0:T(8,128)(2,1)} copy(bf16[128,2048]{1,0:T(8,128)(2,1)} %shard_map.64) | data formatting | bytes 1048576

commit v5 on v4

--- a/solution.py
+++ b/solution.py
@@ -15,6 +15,7 @@
 SCALE2 = HD**-0.5 * LOG2E
 Z = 8
 PLANE = 16
+LATE = 3
 TILES = 16
 CHUNKS = [(0, 4), (9, 3), (4, 5), (12, 4)]
 CROSS_FIRST = sum(tiles for _, tiles in CHUNKS[::2])
@@ -91,16 +92,12 @@
         return e, (z + offset_at(i % Z)) % Z * 2 + (xh + e) % 2
 
     slope = slopes[head] * LOG2E
-    frame_copy.wait()
-    pattern.wait()
 
     def query_frames(i, carry):
         e, row = source(i)
         line = frame_row[(blk + e * (2 - 4 * xl)) * TILES + row].astype(jnp.float32) * slope
         here_all[i] = jnp.broadcast_to(line, (BLOCK, BLOCK)).T
         return carry
-
-    lax.fori_loop(0, TILES, query_frames, 0)
 
     def take(ref, start, tiles, sem):
         view = ref.at[pl.ds(start, tiles)]
@@ -202,7 +199,11 @@
 
     begin, across, along, far, beside, finish = gather(0, k_all)
     value_begin, value_across, value_along, value_far, value_beside, value_finish = gather(1, v_all)
-    begin(0), begin(1), across(0), along(0, False), begin(2), along(1, False), beside(1, 0), along(0, True)
+    begin(0), begin(1)
+    frame_copy.wait()
+    pattern.wait()
+    lax.fori_loop(0, TILES, query_frames, 0)
+    across(0), along(0, False), begin(2), along(1, False), beside(1, 0), along(0, True)
     begin(3), across(2), far(0, False), far(1, False), along(2, False), beside(1, 1), beside(1, 2), far(0, True)
     along(3, False), beside(3, 0), along(2, True), beside(1, 3), far(2, False), far(3, False)
     value_begin(0), value_begin(1)
@@ -212,25 +213,19 @@
     value_begin(2), value_begin(3)
     later = {
         1: [lambda: value_across(0), lambda: value_along(0, False)],
-        3: [lambda: value_along(1, False)],
+        4: [lambda: value_along(1, False)],
         5: [lambda: value_beside(1, 0)],
-        7: [lambda: value_across(2), lambda: value_along(2, False)],
-        10: [lambda: value_along(3, False)],
-        12: [lambda: value_beside(3, 0)],
-        14: [lambda: value_along(0, True)],
-        15: [lambda: value_beside(1, 1)],
-        16: [lambda: value_far(0, False)],
-        17: [lambda: value_far(1, False)],
-        18: [lambda: value_beside(1, 2)],
-        20: [lambda: value_along(2, True)],
-        21: [lambda: value_beside(3, 1)],
-        23: [lambda: value_far(2, False)],
-        24: [lambda: value_far(3, False)],
-        25: [lambda: value_beside(3, 2)],
-        27: [lambda: value_far(0, True)],
-        28: [lambda: value_far(2, True)],
-        29: [lambda: value_beside(1, 3)],
-        31: [lambda: value_beside(3, 3)],
+        8: [lambda: value_across(2), lambda: value_along(2, False)],
+        12: [lambda: value_along(3, False)],
+        13: [lambda: value_beside(3, 0)],
+        16: [lambda: value_along(0, True)],
+        17: [lambda: value_beside(1, 1)],
+        18: [lambda: value_far(0, False)],
+        19: [lambda: value_far(1, False)],
+        20: [lambda: value_beside(1, 2)],
+        23: [lambda: value_along(2, True)],
+        24: [lambda: value_beside(3, 1)],
+        25: [lambda: value_far(2, False)],
     }
 
     def pass_on(i, part):
@@ -242,15 +237,17 @@
                     for step in steps:
                         step()
 
-    def weigh_and_pass(i, carry):
+    def weigh_and_pass(j, carry):
+        i = TILES - 1 - j
         score(i)
-        pass_on(i, 0)
+        pass_on(j, 0)
         weigh(i)
-        pass_on(i, 1)
+        pass_on(j, 1)
         return carry
 
-    lax.fori_loop(0, TILES, weigh_and_pass, 0)
-    value_finish()
+    lax.fori_loop(0, TILES - LATE, weigh_and_pass, 0)
+    value_far(3, False), value_beside(3, 2), value_far(0, True), value_far(2, True), value_beside(1, 3)
+    value_beside(3, 3), value_finish()
 
     def home(i):
         e, dz = i // Z, offset_at(i % Z)
@@ -259,6 +256,12 @@
 
     def block_row(j, carry):
         i = TILES - 1 - j
+
+        @pl.when(i < LATE)
+        def _():
+            score(i)
+            weigh(i)
+
         acc = jnp.zeros((BLOCK, HD), jnp.float32)
         for slot in range(0, width, 2):
             both = jnp.concatenate([v_all[tiles_of[i, slot]], v_all[tiles_of[i, slot + 1]]], axis=0)

time: 101 us -> 100 us (0.990)
  no operation moved by 1% of the time
where the time goes in v5:
time: 100 us; the launch traced here: 99.9 us
  Pallas kernels  98 us (98%)
  local copies, waits for them, and re-layouts  1.88 us (2%)
    pallas_call x1, Pallas kernels, per_device(): pl.pallas_call(functools.partial(kernel, width), out_shape=jax.ShapeDtype...  98 us

profile of v5, /device:TPU:1, one launch (start us, length us, event | category | flops | bytes accessed | tf_op | source)
XLA Modules:
  0.0 99.9 jit_solution(13331415411216082412)
XLA Ops:
  0.0 98.0 %shard_map.64 = bf16[128,2048]{1,0:T(8,128)(2,1)} custom-call(f32[16]{0:T(128)} %slopes.1, s32[16,32,256]{2,1,0:T(8,128)} %bitcast.2, bf16[128,2048]{1,0:T(8,128)(2,1)} %q_hbm.1, bf16[128,2048]{1,0:T(8,128)(2,1)} %k_hbm.1, bf16[128,2048]{1,0:T(8,128)(2,1)} %v_hbm.1, s32[256,1,128]{2,1,0:T(1,128)} %bitcast.3), custom_call_target="tpu_custom_call" | custom-call | tf_op jit(solution)/shard_map/pallas_call | solution.py:297
  98.0 1.9 %copy.8 = bf16[128,2048]{1,0:T(8,128)(2,1)} copy(bf16[128,2048]{1,0:T(8,128)(2,1)} %shard_map.64) | data formatting | bytes 1048576
